TPU v7x, 32 devices: a whole 2x2x4 slice. The times are simulated.
32 devices in a mesh: groups: 1, tm: 32 (over z, y, x, core).
Axes of the slice: x: 2, y: 2, z: 4, core: 2. Of those that a mesh axis runs over, the one named last changes fastest.
Arguments:
- latents: bfloat16 [32, 512, 512], P(('groups', 'tm')), may hold values from -21 to 21
- w_query: bfloat16 [512, 512], replicated, may hold values from -3 to 3
- w_key: bfloat16 [512, 512], replicated, may hold values from -3 to 3
- w_value: bfloat16 [512, 512], replicated, may hold values from -0.25 to 0.25
- w_out: bfloat16 [512, 512], replicated, may hold values from -0.25 to 0.25
- w_time: bfloat16 [3, 512, 512], replicated, may hold values from -0.15625 to 0.15625
- w_space: bfloat16 [3, 3, 512, 512], replicated, may hold values from -0.09375 to 0.09375
- tile_starts: int32 [4], P('groups'), may hold values from 0 to 25, as said below
Outputs:
- decoded: bfloat16 [32, 512, 512], P(('groups', 'tm'))
Inputs may be any that keep to these rules, and one draw needn't show every extreme that they name: `tile_starts`: Increasing; the first is 0, the last is (3) * 8 + 1, and every other start t lies within 2 frames of t * 8.
All inputs are finite; a program needn't handle non-finite values.
Results may differ from a plain program's by a relative error of at most 0.0096.
Values may be sent and summed in bfloat16 or wider, within the bound.
A program may use at most 64 MiB of HBM per device.

v0:
```python
import jax
import jax.numpy as jnp
from jax import lax
from jax.sharding import PartitionSpec as P

PH = 16
PW = 32
OV = 2
epsilon = 1e-06


def passed_along(block, axis, distance):
    devices = range(lax.axis_size(axis))
    route = [(i - distance, i) for i in devices if i - distance in devices]
    return lax.ppermute(block, axis, route)


def rms_norm(array):
    wide = array.astype(jnp.float32)
    return (wide * lax.rsqrt(jnp.mean(wide * wide, axis=-1, keepdims=True) + epsilon)).astype(
        jnp.bfloat16
    )


def project(array, weight):
    extent = array.shape
    product = jnp.dot(array.reshape(-1, extent[-1]), weight, preferred_element_type=jnp.float32)
    return product.reshape(extent[:-1] + (weight.shape[-1],))


def tile_frames(frames, starts):
    reached = starts[None, :] <= frames[:, None]
    new_start = jnp.max(jnp.where(reached, starts[None, :], 0), axis=1)
    earlier = starts[None, :] < new_start[:, None]
    old_start = jnp.max(jnp.where(earlier, starts[None, :], 0), axis=1)
    inside = frames - new_start
    shared = jnp.logical_and(new_start > 0, inside < OV)
    fade = jnp.where(shared, (inside + 1).astype(jnp.float32) / float(OV + 1), jnp.float32(1.0))
    return (new_start, old_start, fade[:, None, None])


def attend(triple):
    queries, key_rows, values = triple
    length = queries.shape[0]
    scale = queries.shape[-1] ** (-0.5)
    scores = (
        jnp.einsum("fipc,gipc->ipfg", queries, key_rows, preferred_element_type=jnp.float32) * scale
    )
    order = jnp.arange(length)
    causal = order[:, None] >= order[None, :]
    scores = jnp.where(causal[None, None], scores, jnp.float32(-1e30))
    peak = jnp.max(scores, axis=-1, keepdims=True)
    expo = jnp.exp(scores - peak)
    weights = (expo / jnp.sum(expo, axis=-1, keepdims=True)).astype(jnp.bfloat16)
    return jnp.einsum(
        "ipfg,gipc->fipc", weights, values, preferred_element_type=jnp.float32
    ).astype(jnp.bfloat16)


def time_blend(padded, frames, starts, w_time):
    length = frames.shape[0]
    extent = padded.shape
    channels = extent[-1]
    flattened = padded.reshape(-1, channels)
    products = [
        jnp.dot(flattened, w_time[lag_index], preferred_element_type=jnp.float32).reshape(
            extent[0], -1, channels
        )
        for lag_index in range(3)
    ]
    new_start, old_start, fade = tile_frames(frames, starts)

    def mixed(context):
        summed = jnp.zeros((length,) + products[0].shape[1:], jnp.float32)
        for lag_index in range(3):
            actual = jnp.minimum(lag_index, frames - context)
            for delta_back in range(lag_index + 1):
                chosen = (actual == delta_back).astype(jnp.float32)[:, None, None]
                summed = (
                    summed + chosen * products[lag_index][2 - delta_back : 2 - delta_back + length]
                )
        return summed

    blended = fade * jax.nn.silu(mixed(new_start)) + (1.0 - fade) * jax.nn.silu(mixed(old_start))
    return blended.astype(jnp.bfloat16)


def space_mix(blended, hidden, w_space):
    length = blended.shape[0]
    channels = blended.shape[-1]
    spatial = blended.reshape(length, PH, PW, channels)
    padded = jnp.pad(spatial, ((0, 0), (1, 1), (1, 1), (0, 0)))
    summed = hidden.reshape(-1, channels).astype(jnp.float32)
    for row_shift in range(3):
        for col_shift in range(3):
            window = padded[:, row_shift : row_shift + PH, col_shift : col_shift + PW].reshape(
                -1, channels
            )
            summed = summed + jnp.dot(
                window, w_space[row_shift, col_shift], preferred_element_type=jnp.float32
            )
    return summed.reshape(length, PH * PW, channels).astype(jnp.bfloat16)


def body(latents, w_query, w_key, w_value, w_out, w_time, w_space, tile_starts):
    frames_dev, row_count, channels = latents.shape
    devices_tm = lax.axis_size("tm")
    share = row_count // devices_tm
    normed = rms_norm(latents).reshape(frames_dev, devices_tm, share, channels)
    queries = project(normed, w_query).astype(jnp.bfloat16)
    key_rows = project(normed, w_key).astype(jnp.bfloat16)
    values = project(normed, w_value).astype(jnp.bfloat16)
    attended = attend(
        (
            lax.all_to_all(queries, "tm", split_axis=1, concat_axis=0, tiled=True),
            lax.all_to_all(key_rows, "tm", split_axis=1, concat_axis=0, tiled=True),
            lax.all_to_all(values, "tm", split_axis=1, concat_axis=0, tiled=True),
        )
    )
    attended = lax.all_to_all(attended, "tm", split_axis=0, concat_axis=1, tiled=True).reshape(
        frames_dev, row_count, channels
    )
    hidden = (latents.astype(jnp.float32) + project(attended, w_out)).astype(jnp.bfloat16)
    smooth = rms_norm(hidden)
    reach = (frames_dev + 1) // frames_dev
    pieces = [passed_along(smooth, "tm", stride) for stride in range(reach, 0, -1)]
    earlier = jnp.concatenate(pieces, axis=0)
    offset = lax.axis_index("tm") * frames_dev
    frames = offset + jnp.arange(frames_dev)
    blended = time_blend(jnp.concatenate([earlier, smooth], axis=0), frames, tile_starts, w_time)
    return space_mix(blended, hidden, w_space)


def solution(mesh):
    placed = (P(("groups", "tm"), None, None), P(), P(), P(), P(), P(), P(), P("groups"))
    return jax.shard_map(
        body, mesh=mesh, in_specs=placed, out_specs=P(("groups", "tm"), None, None), check_vma=False
    )
```

profile of v0, /device:TPU:9, one launch (start us, length us, event | category | flops | bytes accessed | tf_op | source)
XLA Modules:
  0.0 117.2 jit_solution(4229719521326724587)
XLA Ops:
  0.0 0.0 copy-start
  0.0 1.3 %fusion.11 = f32[512]{0:T(512)S(1)} fusion(bf16[1,512,512]{2,1,0:T(8,128)(2,1)} %param.8), kind=kLoop, calls=%fused_computation.33 | loop fusion | flops 785920 | bytes 526336 | tf_op jit(solution)/shard_map/reduce_sum | solution.py:20
  1.3 0.0 copy-start.4
  1.3 1.3 %fusion.12 = bf16[1,512,512]{2,1,0:T(8,128)(2,1)S(1)} fusion(bf16[1,512,512]{2,1,0:T(8,128)(2,1)} %param.8, f32[512]{0:T(512)S(1)} %add_rsqrt_fusion.1), kind=kLoop, calls=%fused_computation.34 | loop fusion | flops 786432 | bytes 1050624 | tf_op jit(solution)/shard_map/convert_element_type | solution.py:20
  2.6 2.3 %fusion.7 = bf16[1,32,16,512]{3,2,0,1:T(8,128)(2,1)} fusion(bf16[32,16,512]{2,1,0:T(8,128)(2,1)S(1)} %bitcast.117, bf16[512,512]{1,0:T(8,128)(2,1)} %param.10), kind=kOutput, calls=%fused_computation.28 | convolution fusion | flops 268697600 | bytes 1572864 | tf_op jit(solution)/shard_map/dot_general | solution.py:27
  4.9 6.4 %all-to-all-start.2 = ((bf16[1,32,16,512]{3,2,0,1:T(8,128)(2,1)}), bf16[1,32,16,512]{3,2,0,1:T(8,128)(2,1)S(1)}, u32[]{:S(2)}, u32[]{:S(2)}) async-start(bf16[1,32,16,512]{3,2,0,1:T(8,128)(2,1)} %fusion.7), calls=%async_computation.2 | async-start | bytes 1048576 | tf_op jit(solution)/shard_map/all_to_all | solution.py:116
  11.2 0.0 copy-done.3
  11.3 1.2 %fusion.6 = bf16[1,32,16,512]{3,2,0,1:T(8,128)(2,1)} fusion(bf16[32,16,512]{2,1,0:T(8,128)(2,1)S(1)} %bitcast.118, bf16[512,512]{1,0:T(8,128)(2,1)S(1)} %copy-done.3), kind=kOutput, calls=%fused_computation.27 | convolution fusion | flops 268697600 | bytes 1572864 | tf_op jit(solution)/shard_map/dot_general | solution.py:27
  12.5 13.0 %all-to-all-done.2 = bf16[1,32,16,512]{3,2,0,1:T(8,128)(2,1)S(1)} async-done(((bf16[1,32,16,512]{3,2,0,1:T(8,128)(2,1)}), bf16[1,32,16,512]{3,2,0,1:T(8,128)(2,1)S(1)}, u32[]{:S(2)}, u32[]{:S(2)}) %all-to-all-start.2) | async-done | bytes 524320 | tf_op jit(solution)/shard_map/all_to_all | solution.py:116
  25.5 4.4 %all-to-all-start.1 = ((bf16[1,32,16,512]{3,2,0,1:T(8,128)(2,1)}), bf16[1,32,16,512]{3,2,0,1:T(8,128)(2,1)S(1)}, u32[]{:S(2)}, u32[]{:S(2)}) async-start(bf16[1,32,16,512]{3,2,0,1:T(8,128)(2,1)} %fusion.6), calls=%async_computation.1 | async-start | bytes 1048576 | tf_op jit(solution)/shard_map/all_to_all | solution.py:115
  29.9 0.0 copy-done.4
  29.9 1.2 %fusion.5 = bf16[1,32,16,512]{3,2,0,1:T(8,128)(2,1)} fusion(bf16[32,16,512]{2,1,0:T(8,128)(2,1)S(1)} %bitcast.119, bf16[512,512]{1,0:T(8,128)(2,1)S(1)} %copy-done.4), kind=kOutput, calls=%fused_computation.26 | convolution fusion | flops 268697600 | bytes 1572864 | tf_op jit(solution)/shard_map/dot_general | solution.py:27
  31.1 13.0 %all-to-all-done.1 = bf16[1,32,16,512]{3,2,0,1:T(8,128)(2,1)S(1)} async-done(((bf16[1,32,16,512]{3,2,0,1:T(8,128)(2,1)}), bf16[1,32,16,512]{3,2,0,1:T(8,128)(2,1)S(1)}, u32[]{:S(2)}, u32[]{:S(2)}) %all-to-all-start.1) | async-done | bytes 524320 | tf_op jit(solution)/shard_map/all_to_all | solution.py:115
  44.1 4.4 %all-to-all-start = ((bf16[1,32,16,512]{3,2,0,1:T(8,128)(2,1)}), bf16[1,32,16,512]{3,2,0,1:T(8,128)(2,1)S(1)}, u32[]{:S(2)}, u32[]{:S(2)}) async-start(bf16[1,32,16,512]{3,2,0,1:T(8,128)(2,1)} %fusion.5), calls=%async_computation | async-start | bytes 1048576 | tf_op jit(solution)/shard_map/all_to_all | solution.py:117
  48.5 0.7 fusion.57
  49.2 13.5 %all-to-all-done = bf16[1,32,16,512]{3,2,0,1:T(8,128)(2,1)S(1)} async-done(((bf16[1,32,16,512]{3,2,0,1:T(8,128)(2,1)}), bf16[1,32,16,512]{3,2,0,1:T(8,128)(2,1)S(1)}, u32[]{:S(2)}, u32[]{:S(2)}) %all-to-all-start) | async-done | bytes 524320 | tf_op jit(solution)/shard_map/all_to_all | solution.py:117
  62.7 0.5 fusion.4
  63.2 0.3 copy.25
  63.5 18.4 %all_to_all.16 = bf16[32,1,16,512]{3,2,1,0:T(8,128)(2,1)S(1)} all-to-all(bf16[32,1,16,512]{3,2,1,0:T(8,128)(2,1)S(1)} %copy.25), channel_id=1, replica_groups=mesh['groups'=1,'tm'=32] {'tm'}, dimensions={0} | all-to-all | bytes 1048576 | tf_op jit(solution)/shard_map/all_to_all | solution.py:120
  82.0 0.0 copy-done
  82.0 0.0 copy-done.1
  82.0 0.5 fusion.13
  82.5 0.2 fusion.14
  82.7 3.0 %collective-permute-start.1 = (bf16[1,512,512]{2,1,0:T(8,128)(2,1)S(1)}, bf16[1,512,512]{2,1,0:T(8,128)(2,1)}, u32[]{:S(2)}, u32[]{:S(2)}) collective-permute-start(bf16[1,512,512]{2,1,0:T(8,128)(2,1)S(1)} %fusion.14), channel_id=1, source_target_pairs={{0,1},{1,2},{2,3},{3,4},{4,5},{5,6},{6,7},{7,8},{8,9},{9,10},{10,1... | collective-permute-start | bytes 1572872 | tf_op jit(solution)/shard_map/ppermute | solution.py:15
  85.7 3.6 %collective-permute-start = (bf16[1,512,512]{2,1,0:T(8,128)(2,1)S(1)}, bf16[1,512,512]{2,1,0:T(8,128)(2,1)}, u32[]{:S(2)}, u32[]{:S(2)}) collective-permute-start(bf16[1,512,512]{2,1,0:T(8,128)(2,1)S(1)} %fusion.14), channel_id=1, source_target_pairs={{0,2},{1,3},{2,4},{3,5},{4,6},{5,7},{6,8},{7,9},{8,10},{9,11},{10,... | collective-permute-start | bytes 1572872 | tf_op jit(solution)/shard_map/ppermute | solution.py:15
  89.3 0.0 copy-done.5
  89.3 0.6 fusion.55
  89.9 1.2 %fusion.56 = s32[]{:T(128)} fusion(s32[4]{0:T(128)S(1)} %copy-done.5, s32[]{:T(128)} %fusion.55), kind=kLoop, calls=%fused_computation.91 | loop fusion | flops 11 | bytes 24 | tf_op jit(solution)/shard_map/reduce_max | solution.py:35
  93.1 1.3 %collective-permute-done.1 = bf16[1,512,512]{2,1,0:T(8,128)(2,1)} collective-permute-done((bf16[1,512,512]{2,1,0:T(8,128)(2,1)S(1)}, bf16[1,512,512]{2,1,0:T(8,128)(2,1)}, u32[]{:S(2)}, u32[]{:S(2)}) %collective-permute-start.1) | collective-permute-done | bytes 524320 | tf_op jit(solution)/shard_map/ppermute | solution.py:15
  94.4 12.5 %collective-permute-done = bf16[1,512,512]{2,1,0:T(8,128)(2,1)} collective-permute-done((bf16[1,512,512]{2,1,0:T(8,128)(2,1)S(1)}, bf16[1,512,512]{2,1,0:T(8,128)(2,1)}, u32[]{:S(2)}, u32[]{:S(2)}) %collective-permute-start) | collective-permute-done | bytes 524320 | tf_op jit(solution)/shard_map/ppermute | solution.py:15
  106.9 1.4 %pad_maximum_fusion = bf16[3,512,512]{2,1,0:T(8,128)(2,1)S(1)} fusion(bf16[1,512,512]{2,1,0:T(8,128)(2,1)S(1)} %fusion.14, bf16[1,512,512]{2,1,0:T(8,128)(2,1)} %collective-permute-done.1, bf16[1,512,512]{2,1,0:T(8,128)(2,1)} %collective-permute-done), kind=kLoop, calls=%fused_computation.1 | loop fusion | flops 1572864 | bytes 3145728 | tf_op jit(solution)/shard_map/concatenate | solution.py:130
  108.2 0.0 copy-done.2
  108.2 1.0 fusion.28
  109.2 0.0 slice-start
  109.2 1.0 fusion.30
  110.2 0.0 slice-start.1
  110.2 1.5 %add_convert_fusion = bf16[512,512]{1,0:T(8,128)(2,1)S(1)} fusion(f32[1536,512]{1,0:T(8,128)S(1)} %fusion.28, f32[1536,512]{1,0:T(8,128)S(1)} %fusion.30, bf16[1536,512]{1,0:T(8,128)(2,1)S(1)} %bitcast.116, f32[]{:T(128)S(6)} %sub.31, f32[]{:T(128)S(6)} %select_n.22, f32[]{:T(128)S(6)} %convert_element_type.146, f32[]{:T(128)S(6)} %convert_element_type.145, ...), kind=kOutput, calls=%fused_computation.37 | convolution fusion | flops 277348352 | bytes 6815800 | tf_op jit(solution)/shard_map/dot_general | solution.py:66
  111.8 0.7 pad_slice_fusion
  112.4 0.0 slice-done
  112.5 0.4 convolution_add_fusion.8
  112.9 0.4 convolution_add_fusion.7
  113.3 0.4 convolution_add_fusion.6
  113.8 0.4 convolution_add_fusion.5
  114.2 0.4 convolution_add_fusion.4
  114.7 0.4 convolution_add_fusion.3
  115.1 0.4 convolution_add_fusion.2
  115.6 0.4 convolution_add_fusion.1
  116.0 1.2 %fusion.3 = bf16[1,512,512]{2,1,0:T(8,128)(2,1)} fusion(f32[512,512]{1,0:T(8,128)S(1)} %convolution_add_fusion.1, bf16[512,512]{1,0:T(8,128)(2,1)S(1)} %bitcast.122, bf16[3,3,512,512]{3,2,1,0:T(8,128)(2,1)S(1)} %bitcast.121), kind=kOutput, calls=%fused_computation.24 | convolution fusion | flops 268959744 | bytes 2621440 | tf_op jit(solution)/shard_map/dot_general | solution.py:99
  (9 shorter events, 0.0 us)
Async XLA Ops:
  0.0 82.0 %copy-start = (bf16[512,512]{1,0:T(8,128)(2,1)S(1)}, bf16[512,512]{1,0:T(8,128)(2,1)}, u32[]{:S(2)}) copy-start(bf16[512,512]{1,0:T(8,128)(2,1)} %param.12) | copy-start | bytes 1572868
  0.0 11.2 %copy-start.3 = (bf16[512,512]{1,0:T(8,128)(2,1)S(1)}, bf16[512,512]{1,0:T(8,128)(2,1)}, u32[]{:S(2)}) copy-start(bf16[512,512]{1,0:T(8,128)(2,1)} %param.9) | copy-start | bytes 1572868
  1.3 28.6 %copy-start.4 = (bf16[512,512]{1,0:T(8,128)(2,1)S(1)}, bf16[512,512]{1,0:T(8,128)(2,1)}, u32[]{:S(2)}) copy-start(bf16[512,512]{1,0:T(8,128)(2,1)} %param.11) | copy-start | bytes 1572868
  4.9 20.6 %all-to-all-start.2 = ((bf16[1,32,16,512]{3,2,0,1:T(8,128)(2,1)}), bf16[1,32,16,512]{3,2,0,1:T(8,128)(2,1)S(1)}, u32[]{:S(2)}, u32[]{:S(2)}) async-start(bf16[1,32,16,512]{3,2,0,1:T(8,128)(2,1)} %fusion.7), calls=%async_computation.2 | async-start | bytes 1048576 | tf_op jit(solution)/shard_map/all_to_all | solution.py:116
  25.5 18.6 %all-to-all-start.1 = ((bf16[1,32,16,512]{3,2,0,1:T(8,128)(2,1)}), bf16[1,32,16,512]{3,2,0,1:T(8,128)(2,1)S(1)}, u32[]{:S(2)}, u32[]{:S(2)}) async-start(bf16[1,32,16,512]{3,2,0,1:T(8,128)(2,1)} %fusion.6), calls=%async_computation.1 | async-start | bytes 1048576 | tf_op jit(solution)/shard_map/all_to_all | solution.py:115
  31.1 50.9 %copy-start.1 = (bf16[1,512,512]{2,1,0:T(8,128)(2,1)S(1)}, bf16[1,512,512]{2,1,0:T(8,128)(2,1)}, u32[]{:S(2)}) copy-start(bf16[1,512,512]{2,1,0:T(8,128)(2,1)} %param.8) | copy-start | bytes 1572868
  44.1 18.6 %all-to-all-start = ((bf16[1,32,16,512]{3,2,0,1:T(8,128)(2,1)}), bf16[1,32,16,512]{3,2,0,1:T(8,128)(2,1)S(1)}, u32[]{:S(2)}, u32[]{:S(2)}) async-start(bf16[1,32,16,512]{3,2,0,1:T(8,128)(2,1)} %fusion.5), calls=%async_computation | async-start | bytes 1048576 | tf_op jit(solution)/shard_map/all_to_all | solution.py:117
  63.2 26.1 %copy-start.5 = (s32[4]{0:T(128)S(1)}, s32[4]{0:T(128)}, u32[]{:S(2)}) copy-start(s32[4]{0:T(128)} %param.15) | copy-start | bytes 52
  82.0 26.3 %copy-start.2 = (bf16[3,512,512]{2,1,0:T(8,128)(2,1)S(1)}, bf16[3,512,512]{2,1,0:T(8,128)(2,1)}, u32[]{:S(2)}) copy-start(bf16[3,512,512]{2,1,0:T(8,128)(2,1)} %param.13) | copy-start | bytes 4718596
  82.7 11.7 %collective-permute-start.1 = (bf16[1,512,512]{2,1,0:T(8,128)(2,1)S(1)}, bf16[1,512,512]{2,1,0:T(8,128)(2,1)}, u32[]{:S(2)}, u32[]{:S(2)}) collective-permute-start(bf16[1,512,512]{2,1,0:T(8,128)(2,1)S(1)} %fusion.14), channel_id=1, source_target_pairs={{0,1},{1,2},{2,3},{3,4},{4,5},{5,6},{6,7},{7,8},{8,9},{9,10},{10,1... | collective-permute-start | bytes 1572872 | tf_op jit(solution)/shard_map/ppermute | solution.py:15
  85.7 21.1 %collective-permute-start = (bf16[1,512,512]{2,1,0:T(8,128)(2,1)S(1)}, bf16[1,512,512]{2,1,0:T(8,128)(2,1)}, u32[]{:S(2)}, u32[]{:S(2)}) collective-permute-start(bf16[1,512,512]{2,1,0:T(8,128)(2,1)S(1)} %fusion.14), channel_id=1, source_target_pairs={{0,2},{1,3},{2,4},{3,5},{4,6},{5,7},{6,8},{7,9},{8,10},{9,11},{10,... | collective-permute-start | bytes 1572872 | tf_op jit(solution)/shard_map/ppermute | solution.py:15
  109.2 3.2 %slice-start = ((s8[4718592]{0:T(1024)(128)(4,1)}), s8[4194304]{0:T(1024)(128)(4,1)S(1)}, s32[]{:S(2)}) async-start(s8[4718592]{0:T(1024)(128)(4,1)} %bitcast.120), calls=%async_computation.4 | async-start | bytes 8388608
  110.2 2.2 %slice-start.1 = ((s8[4718592]{0:T(1024)(128)(4,1)}), s8[524288]{0:T(1024)(128)(4,1)S(1)}, s32[]{:S(2)}) async-start(s8[4718592]{0:T(1024)(128)(4,1)} %bitcast.120), calls=%async_computation.5 | async-start | bytes 1048576
where the time goes:
time: 118 us; the launch traced here: 117 us
  waiting for transfers between devices  53.1 us (45%)
  starting transfers between devices  21.8 us (18%)
  blocking collectives  18.4 us (16%)
  matrix products  14.7 us (12%)
  other arithmetic  6.02 us (5%)
  between operations  2.18 us (2%)
    all_to_all x1, blocking collectives, body(): lax.all_to_all(attended, 'tm', split_axis=0, concat_axis=1, tiled=True)  18.4 us
    ppermute x2, waiting for transfers between devices, passed_along(): return lax.ppermute(block, axis, route)  13.7 us
    all_to_all x1, waiting for transfers between devices, body(): lax.all_to_all(values, 'tm', split_axis=1, concat_axis=0, tiled=True)  13.5 us
    all_to_all x1, waiting for transfers between devices, body(): lax.all_to_all(key_rows, 'tm', split_axis=1, concat_axis=0, tiled=True)  13 us
    all_to_all x1, waiting for transfers between devices, body(): lax.all_to_all(queries, 'tm', split_axis=1, concat_axis=0, tiled=True)  13 us
    ppermute x2, starting transfers between devices, passed_along(): return lax.ppermute(block, axis, route)  6.57 us
    all_to_all x1, starting transfers between devices, body(): lax.all_to_all(key_rows, 'tm', split_axis=1, concat_axis=0, tiled=True)  6.36 us
    dot_general x4, matrix products, project(): jnp.dot(array.reshape(-1, extent[-1]), weight, preferred_element_type=jnp...  5.27 us
  transfers between devices with their start and end apart: 5, of which 5 were waited for; matrix products, arithmetic and copies ran while one was open for 4% of the time, Pallas kernels for 0%

commit v1 on v0

--- a/solution.py
+++ b/solution.py
@@ -7,6 +7,13 @@
 PW = 32
 OV = 2
 epsilon = 1e-06
+
+
+def swap_blocks(block, mesh_axis, split, join):
+    size = lax.axis_size(mesh_axis)
+    shards = jnp.stack(jnp.split(block, size, axis=split), axis=0)
+    shards = lax.all_to_all(shards, mesh_axis, split_axis=0, concat_axis=0)
+    return jnp.concatenate(shards, axis=join)
 
 
 def passed_along(block, axis, distance):
@@ -112,7 +119,7 @@
     values = project(normed, w_value).astype(jnp.bfloat16)
     attended = attend(
         (
-            lax.all_to_all(queries, "tm", split_axis=1, concat_axis=0, tiled=True),
+            swap_blocks(queries, "tm", 1, 0),
             lax.all_to_all(key_rows, "tm", split_axis=1, concat_axis=0, tiled=True),
             lax.all_to_all(values, "tm", split_axis=1, concat_axis=0, tiled=True),
         )

time: 118 us -> 136 us (1.15)
  local copies, waits for them, and re-layouts: 0.99 us -> 20.4 us
    unnamed x16 -> x47, local copies, waits for them, and re-layouts: 0.04 us -> 18.8 us
    all_to_all x1, starting transfers between devices: 4.42 us -> 6.36 us  [swap_blocks(): shards = lax.all_to_all(shards, mesh_axis, split_axis=0, concat_axis=0)]
    all_to_all x1, starting transfers between devices: 6.36 us -> 4.42 us  [body(): lax.all_to_all(key_rows, 'tm', split_axis=1, concat_axis=0, tiled=True)]
where the time goes in v1:
time: 136 us
  waiting for transfers between devices  53.1 us (39%)
  starting transfers between devices  21.8 us (16%)
  local copies, waits for them, and re-layouts  20.4 us (15%)
  blocking collectives  18.4 us (14%)
  matrix products  14 us (10%)
  other arithmetic  5.97 us (4%)
  between operations  2.21 us (2%)
    unnamed x47, local copies, waits for them, and re-layouts  18.8 us
    all_to_all x1, blocking collectives, body(): lax.all_to_all(attended, 'tm', split_axis=0, concat_axis=1, tiled=True)  18.4 us
    ppermute x2, waiting for transfers between devices, passed_along(): return lax.ppermute(block, axis, route)  13.7 us
    all_to_all x1, waiting for transfers between devices, body(): lax.all_to_all(values, 'tm', split_axis=1, concat_axis=0, tiled=True)  13.5 us
    all_to_all x1, waiting for transfers between devices, swap_blocks(): shards = lax.all_to_all(shards, mesh_axis, split_axis=0, concat_axis=0)  13 us
    all_to_all x1, waiting for transfers between devices, body(): lax.all_to_all(key_rows, 'tm', split_axis=1, concat_axis=0, tiled=True)  13 us
    ppermute x2, starting transfers between devices, passed_along(): return lax.ppermute(block, axis, route)  6.57 us
    all_to_all x1, starting transfers between devices, swap_blocks(): shards = lax.all_to_all(shards, mesh_axis, split_axis=0, concat_axis=0)  6.36 us
  transfers between devices with their start and end apart: 5, of which 5 were waited for; matrix products, arithmetic and copies ran while one was open for 4% of the time, Pallas kernels for 0%

profile of v1, /device:TPU:9, one launch (start us, length us, event | category | flops | bytes accessed | tf_op | source)
XLA Modules:
  0.0 135.9 jit_solution(15416567641050121901)
XLA Ops:
  0.0 1.3 fusion.11
  1.3 1.2 fusion.12
  2.5 1.5 %fusion.6 = bf16[1,32,16,512]{3,2,1,0:T(8,128)(2,1)S(1)} fusion(bf16[32,16,512]{2,1,0:T(8,128)(2,1)S(1)} %bitcast.239, bf16[512,512]{1,0:T(8,128)(2,1)} %param.9), kind=kOutput, calls=%fused_computation.27 | convolution fusion | flops 268697600 | bytes 1572864 | tf_op jit(solution)/shard_map/dot_general | solution.py:34
  4.1 0.6 constant_dynamic-update-slice_fusion.31
  5.9 0.6 constant_dynamic-update-slice_fusion.28
  6.5 0.6 constant_dynamic-update-slice_fusion.27
  7.1 0.6 constant_dynamic-update-slice_fusion.26
  7.7 0.6 constant_dynamic-update-slice_fusion.25
  8.3 0.6 constant_dynamic-update-slice_fusion.24
  8.9 0.6 constant_dynamic-update-slice_fusion.23
  9.6 0.6 constant_dynamic-update-slice_fusion.22
  10.2 0.6 constant_dynamic-update-slice_fusion.21
  12.0 0.6 constant_dynamic-update-slice_fusion.18
  12.6 0.6 constant_dynamic-update-slice_fusion.17
  13.2 0.6 constant_dynamic-update-slice_fusion.16
  13.8 0.6 constant_dynamic-update-slice_fusion.15
  14.4 0.6 constant_dynamic-update-slice_fusion.14
  15.0 0.6 constant_dynamic-update-slice_fusion.13
  15.6 0.6 constant_dynamic-update-slice_fusion.12
  17.4 0.6 constant_dynamic-update-slice_fusion.9
  18.0 0.6 constant_dynamic-update-slice_fusion.8
  18.7 0.6 constant_dynamic-update-slice_fusion.7
  19.3 0.6 constant_dynamic-update-slice_fusion.6
  19.9 0.6 constant_dynamic-update-slice_fusion.5
  20.5 0.6 constant_dynamic-update-slice_fusion.4
  21.1 0.6 constant_dynamic-update-slice_fusion.3
  23.5 6.4 %all-to-all-start.1 = ((bf16[32,1,1,16,512]{4,3,2,1,0:T(8,128)(2,1)}), bf16[32,1,1,16,512]{4,3,2,1,0:T(8,128)(2,1)S(1)}, u32[]{:S(2)}, u32[]{:S(2)}) async-start(bf16[32,1,1,16,512]{4,3,2,1,0:T(8,128)(2,1)} %constant_dynamic-update-slice_fusion), calls=%async_computation.1 | async-start | bytes 1048576 | tf_op jit(solution)/shard_map/all_to_all | solution.py:15
  29.9 1.2 fusion.7
  31.1 13.0 %all-to-all-done.1 = bf16[32,1,1,16,512]{4,3,2,1,0:T(8,128)(2,1)S(1)} async-done(((bf16[32,1,1,16,512]{4,3,2,1,0:T(8,128)(2,1)}), bf16[32,1,1,16,512]{4,3,2,1,0:T(8,128)(2,1)S(1)}, u32[]{:S(2)}, u32[]{:S(2)}) %all-to-all-start.1) | async-done | bytes 524320 | tf_op jit(solution)/shard_map/all_to_all | solution.py:15
  44.1 4.4 %all-to-all-start.2 = ((bf16[1,32,16,512]{3,2,0,1:T(8,128)(2,1)}), bf16[1,32,16,512]{3,2,0,1:T(8,128)(2,1)S(1)}, u32[]{:S(2)}, u32[]{:S(2)}) async-start(bf16[1,32,16,512]{3,2,0,1:T(8,128)(2,1)} %fusion.7), calls=%async_computation.2 | async-start | bytes 1048576 | tf_op jit(solution)/shard_map/all_to_all | solution.py:123
  48.5 1.2 fusion.5
  49.8 13.0 %all-to-all-done.2 = bf16[1,32,16,512]{3,2,0,1:T(8,128)(2,1)S(1)} async-done(((bf16[1,32,16,512]{3,2,0,1:T(8,128)(2,1)}), bf16[1,32,16,512]{3,2,0,1:T(8,128)(2,1)S(1)}, u32[]{:S(2)}, u32[]{:S(2)}) %all-to-all-start.2) | async-done | bytes 524320 | tf_op jit(solution)/shard_map/all_to_all | solution.py:123
  62.7 4.4 %all-to-all-start = ((bf16[1,32,16,512]{3,2,0,1:T(8,128)(2,1)}), bf16[1,32,16,512]{3,2,0,1:T(8,128)(2,1)S(1)}, u32[]{:S(2)}, u32[]{:S(2)}) async-start(bf16[1,32,16,512]{3,2,0,1:T(8,128)(2,1)} %fusion.5), calls=%async_computation | async-start | bytes 1048576 | tf_op jit(solution)/shard_map/all_to_all | solution.py:124
  67.1 0.7 fusion.56
  67.9 13.5 %all-to-all-done = bf16[1,32,16,512]{3,2,0,1:T(8,128)(2,1)S(1)} async-done(((bf16[1,32,16,512]{3,2,0,1:T(8,128)(2,1)}), bf16[1,32,16,512]{3,2,0,1:T(8,128)(2,1)S(1)}, u32[]{:S(2)}, u32[]{:S(2)}) %all-to-all-start) | async-done | bytes 524320 | tf_op jit(solution)/shard_map/all_to_all | solution.py:124
  82.2 18.4 %all_to_all.32 = bf16[32,1,16,512]{3,2,1,0:T(8,128)(2,1)S(1)} all-to-all(bf16[32,1,16,512]{3,2,1,0:T(8,128)(2,1)S(1)} %copy.24), channel_id=1, replica_groups=mesh['groups'=1,'tm'=32] {'tm'}, dimensions={0} | all-to-all | bytes 1048576 | tf_op jit(solution)/shard_map/all_to_all | solution.py:127
  101.3 3.0 %collective-permute-start.1 = (bf16[1,512,512]{2,1,0:T(8,128)(2,1)S(1)}, bf16[1,512,512]{2,1,0:T(8,128)(2,1)}, u32[]{:S(2)}, u32[]{:S(2)}) collective-permute-start(bf16[1,512,512]{2,1,0:T(8,128)(2,1)S(1)} %fusion.14), channel_id=1, source_target_pairs={{0,1},{1,2},{2,3},{3,4},{4,5},{5,6},{6,7},{7,8},{8,9},{9,10},{10,1... | collective-permute-start | bytes 1572872 | tf_op jit(solution)/shard_map/ppermute | solution.py:22
  104.4 3.6 %collective-permute-start = (bf16[1,512,512]{2,1,0:T(8,128)(2,1)S(1)}, bf16[1,512,512]{2,1,0:T(8,128)(2,1)}, u32[]{:S(2)}, u32[]{:S(2)}) collective-permute-start(bf16[1,512,512]{2,1,0:T(8,128)(2,1)S(1)} %fusion.14), channel_id=1, source_target_pairs={{0,2},{1,3},{2,4},{3,5},{4,6},{5,7},{6,8},{7,9},{8,10},{9,11},{10,... | collective-permute-start | bytes 1572872 | tf_op jit(solution)/shard_map/ppermute | solution.py:22
  107.9 0.6 fusion.54
  108.6 1.2 fusion.55
  111.8 1.3 collective-permute-done.1
  113.0 12.5 %collective-permute-done = bf16[1,512,512]{2,1,0:T(8,128)(2,1)} collective-permute-done((bf16[1,512,512]{2,1,0:T(8,128)(2,1)S(1)}, bf16[1,512,512]{2,1,0:T(8,128)(2,1)}, u32[]{:S(2)}, u32[]{:S(2)}) %collective-permute-start) | collective-permute-done | bytes 524320 | tf_op jit(solution)/shard_map/ppermute | solution.py:22
  125.5 1.4 %pad_maximum_fusion = bf16[3,512,512]{2,1,0:T(8,128)(2,1)S(1)} fusion(bf16[1,512,512]{2,1,0:T(8,128)(2,1)S(1)} %fusion.14, bf16[1,512,512]{2,1,0:T(8,128)(2,1)} %collective-permute-done.1, bf16[1,512,512]{2,1,0:T(8,128)(2,1)} %collective-permute-done), kind=kLoop, calls=%fused_computation.1 | loop fusion | flops 1572864 | bytes 3145728 | tf_op jit(solution)/shard_map/concatenate | solution.py:137
  126.9 1.0 fusion.28
  127.9 1.0 fusion.30
  128.9 1.5 %add_convert_fusion = bf16[512,512]{1,0:T(8,128)(2,1)S(1)} fusion(f32[1536,512]{1,0:T(8,128)S(1)} %fusion.28, f32[1536,512]{1,0:T(8,128)S(1)} %fusion.30, bf16[1536,512]{1,0:T(8,128)(2,1)S(1)} %bitcast.238, f32[]{:T(128)S(6)} %sub.31, f32[]{:T(128)S(6)} %select_n.22, f32[]{:T(128)S(6)} %convert_element_type.146, f32[]{:T(128)S(6)} %convert_element_type.145, ...), kind=kOutput, calls=%fused_computation.37 | convolution fusion | flops 277348352 | bytes 6815800 | tf_op jit(solution)/shard_map/dot_general | solution.py:73
  130.4 0.7 pad_slice_fusion
  134.6 1.2 fusion.3
  (41 shorter events, 10.5 us)
Async XLA Ops:
  0.0 100.6 %copy-start = (bf16[512,512]{1,0:T(8,128)(2,1)S(1)}, bf16[512,512]{1,0:T(8,128)(2,1)}, u32[]{:S(2)}) copy-start(bf16[512,512]{1,0:T(8,128)(2,1)} %param.12) | copy-start | bytes 1572868
  0.0 29.9 %copy-start.3 = (bf16[512,512]{1,0:T(8,128)(2,1)S(1)}, bf16[512,512]{1,0:T(8,128)(2,1)}, u32[]{:S(2)}) copy-start(bf16[512,512]{1,0:T(8,128)(2,1)} %param.10) | copy-start | bytes 1572868
  2.5 46.0 %copy-start.4 = (bf16[512,512]{1,0:T(8,128)(2,1)S(1)}, bf16[512,512]{1,0:T(8,128)(2,1)}, u32[]{:S(2)}) copy-start(bf16[512,512]{1,0:T(8,128)(2,1)} %param.11) | copy-start | bytes 1572868
  23.5 20.6 %all-to-all-start.1 = ((bf16[32,1,1,16,512]{4,3,2,1,0:T(8,128)(2,1)}), bf16[32,1,1,16,512]{4,3,2,1,0:T(8,128)(2,1)S(1)}, u32[]{:S(2)}, u32[]{:S(2)}) async-start(bf16[32,1,1,16,512]{4,3,2,1,0:T(8,128)(2,1)} %constant_dynamic-update-slice_fusion), calls=%async_computation.1 | async-start | bytes 1048576 | tf_op jit(solution)/shard_map/all_to_all | solution.py:15
  44.1 18.6 %all-to-all-start.2 = ((bf16[1,32,16,512]{3,2,0,1:T(8,128)(2,1)}), bf16[1,32,16,512]{3,2,0,1:T(8,128)(2,1)S(1)}, u32[]{:S(2)}, u32[]{:S(2)}) async-start(bf16[1,32,16,512]{3,2,0,1:T(8,128)(2,1)} %fusion.7), calls=%async_computation.2 | async-start | bytes 1048576 | tf_op jit(solution)/shard_map/all_to_all | solution.py:123
  49.7 50.9 %copy-start.1 = (bf16[1,512,512]{2,1,0:T(8,128)(2,1)S(1)}, bf16[1,512,512]{2,1,0:T(8,128)(2,1)}, u32[]{:S(2)}) copy-start(bf16[1,512,512]{2,1,0:T(8,128)(2,1)} %param.8) | copy-start | bytes 1572868
  62.7 18.6 %all-to-all-start = ((bf16[1,32,16,512]{3,2,0,1:T(8,128)(2,1)}), bf16[1,32,16,512]{3,2,0,1:T(8,128)(2,1)S(1)}, u32[]{:S(2)}, u32[]{:S(2)}) async-start(bf16[1,32,16,512]{3,2,0,1:T(8,128)(2,1)} %fusion.5), calls=%async_computation | async-start | bytes 1048576 | tf_op jit(solution)/shard_map/all_to_all | solution.py:124
  81.9 26.1 %copy-start.5 = (s32[4]{0:T(128)S(1)}, s32[4]{0:T(128)}, u32[]{:S(2)}) copy-start(s32[4]{0:T(128)} %param.15) | copy-start | bytes 52
  100.6 26.3 %copy-start.2 = (bf16[3,512,512]{2,1,0:T(8,128)(2,1)S(1)}, bf16[3,512,512]{2,1,0:T(8,128)(2,1)}, u32[]{:S(2)}) copy-start(bf16[3,512,512]{2,1,0:T(8,128)(2,1)} %param.13) | copy-start | bytes 4718596
  101.3 11.7 %collective-permute-start.1 = (bf16[1,512,512]{2,1,0:T(8,128)(2,1)S(1)}, bf16[1,512,512]{2,1,0:T(8,128)(2,1)}, u32[]{:S(2)}, u32[]{:S(2)}) collective-permute-start(bf16[1,512,512]{2,1,0:T(8,128)(2,1)S(1)} %fusion.14), channel_id=1, source_target_pairs={{0,1},{1,2},{2,3},{3,4},{4,5},{5,6},{6,7},{7,8},{8,9},{9,10},{10,1... | collective-permute-start | bytes 1572872 | tf_op jit(solution)/shard_map/ppermute | solution.py:22
  104.4 21.1 %collective-permute-start = (bf16[1,512,512]{2,1,0:T(8,128)(2,1)S(1)}, bf16[1,512,512]{2,1,0:T(8,128)(2,1)}, u32[]{:S(2)}, u32[]{:S(2)}) collective-permute-start(bf16[1,512,512]{2,1,0:T(8,128)(2,1)S(1)} %fusion.14), channel_id=1, source_target_pairs={{0,2},{1,3},{2,4},{3,5},{4,6},{5,7},{6,8},{7,9},{8,10},{9,11},{10,... | collective-permute-start | bytes 1572872 | tf_op jit(solution)/shard_map/ppermute | solution.py:22
  127.9 3.2 %slice-start = ((s8[4718592]{0:T(1024)(128)(4,1)}), s8[4194304]{0:T(1024)(128)(4,1)S(1)}, s32[]{:S(2)}) async-start(s8[4718592]{0:T(1024)(128)(4,1)} %bitcast.242), calls=%async_computation.4 | async-start | bytes 8388608
  128.8 2.2 %slice-start.1 = ((s8[4718592]{0:T(1024)(128)(4,1)}), s8[524288]{0:T(1024)(128)(4,1)S(1)}, s32[]{:S(2)}) async-start(s8[4718592]{0:T(1024)(128)(4,1)} %bitcast.242), calls=%async_computation.5 | async-start | bytes 1048576
